TPU v7x, 32 devices: a whole 2x2x4 slice. The times are simulated.
32 devices in a mesh: groups: 2 (over x), pages: 16 (over z, y, core).
Axes of the slice: x: 2, y: 2, z: 4, core: 2. Of those that a mesh axis runs over, the one named last changes fastest.
Arguments:
- queries: bfloat16 [2, 512, 8192], P(None, 'groups'), parts along dimension 1, may hold values from -14 to 14
- kv_cache: bfloat16 [256, 128, 2, 1024], P(('groups', 'pages')), parts along dimension 0, may hold values from -14 to 14
- w_out: bfloat16 [8192, 8192], P('pages'), may hold values from -0.0625 to 0.0625
- slot_page_before: int32 [256], P(('groups', 'pages')), parts along dimension 0, may hold values from -1 to 127, as said below
- slot_page_after: int32 [256], P(('groups', 'pages')), parts along dimension 0, may hold values from -1 to 127, as said below
- move_out: int32 [32, 4], P(('groups', 'pages')), parts along dimension 0, may hold values from -1 to 7, as said below
- move_in: int32 [32, 4], P(('groups', 'pages')), parts along dimension 0, may hold values from -1 to 7, as said below
- positions: int32 [2, 512], P(None, 'groups'), parts along dimension 1, may hold values from 0 to 16383, as said below
Outputs:
- attn_output: bfloat16 [2, 512, 8192], P(None, ('groups', 'pages')), parts along dimension 1
- cache_after: bfloat16 [256, 128, 2, 1024], P(('groups', 'pages')), parts along dimension 0
There are 2 independent parts, one for each index of `groups`. A program takes and returns all parts, laid end to end along the dimension named above; an argument that names none is the same for every part. Nothing has to cross between parts.
Inputs may be any that keep to these rules, and one draw needn't show every extreme that they name: `slot_page_before`: the logical page held by each slot; -1 marks a free slot; the live pages are the last ones of the sequence, numbered consecutively up to 127, each in exactly one slot; an owner's free slots are its last ones. `slot_page_after`: pages that are not sent keep their slot, each sent page sits in the slot that move_in names at its new owner, and a slot that sent its page is free. `move_out`: entry [j, o - 1] is a slot of owner j holding a live page, sent to owner (j + o) mod 16, or -1; the slots of one row differ; an owner sends at most one page to each of its next 4 owners. `move_in`: entry [j, o - 1] is a slot of owner j that is free before the moves, or -1, which it is exactly where move_out[(j - o) mod 16, o - 1] is -1; the slots of one row differ. Each row holds 256 consecutive positions; row 1 ends at the last position of the last live page; at most 256 positions lie between the end of row 0 and the start of row 1; all lie within the live pages.
All inputs are finite; a program needn't handle non-finite values.
Results may differ from a plain program's by a relative error of at most 0.0055.
Values may be sent and summed in bfloat16 or wider, within the bound.
No kernel may reach another device: no remote copies, remote signals or barrier semaphores. Data moves between devices by JAX's collectives and lax.ppermute only.
A program may use at most 192 MiB of HBM per device.

v0:
```python
import jax
import jax.numpy as jnp
from jax import lax
from jax.sharding import PartitionSpec as P

HEADS = 64
KV_HEADS = 8
HEAD_DIM = 128
D = 8192
PAGE_TOK = 128
BLOCK = 256
MOVE_WIN = 4
floor_score = -1e30


def passed_along(block, axis, distance):
    devices = range(lax.axis_size(axis))
    route = [((i - distance) % len(devices), i) for i in devices]
    return lax.ppermute(block, axis, route)


def block_partials(query_rows, cache_rows, slot_table, positions_row):
    key_count = cache_rows.shape[0] * PAGE_TOK
    head_group = HEADS // KV_HEADS
    key_rows = cache_rows[:, :, 0, :].reshape(key_count, KV_HEADS, HEAD_DIM)
    value_rows = cache_rows[:, :, 1, :].reshape(key_count, KV_HEADS, HEAD_DIM)
    key_pos = (
        slot_table[:, None] * PAGE_TOK + jnp.arange(PAGE_TOK, dtype=jnp.int32)[None, :]
    ).reshape(key_count)
    live_keys = jnp.repeat(slot_table >= 0, PAGE_TOK)
    sub_rows = min(64, BLOCK)
    score_scale = HEAD_DIM ** (-0.5)
    queries_in = query_rows.reshape(BLOCK // sub_rows, sub_rows, KV_HEADS, head_group, HEAD_DIM)
    places = positions_row.reshape(BLOCK // sub_rows, sub_rows)

    def one_block(inputs):
        query_block, query_pos = inputs
        scores = (
            jnp.einsum("qhgd,khd->qhgk", query_block, key_rows, preferred_element_type=jnp.float32)
            * score_scale
        )
        visible = (live_keys[None, :] & (key_pos[None, :] <= query_pos[:, None]))[:, None, None, :]
        scores = jnp.where(visible, scores, floor_score)
        row_max = jnp.max(scores, axis=-1)
        weights = jnp.where(visible, jnp.exp(scores - row_max[..., None]), 0.0).astype(jnp.bfloat16)
        row_sum = jnp.sum(weights, axis=-1, dtype=jnp.float32)
        mixed_rows = jnp.einsum(
            "qhgk,khd->qhgd", weights, value_rows, preferred_element_type=jnp.float32
        )
        return (
            mixed_rows.reshape(sub_rows, HEADS * HEAD_DIM),
            row_max.reshape(sub_rows, HEADS),
            row_sum.reshape(sub_rows, HEADS),
        )

    mixed_rows, row_max, row_sum = lax.map(one_block, (queries_in, places))
    return (
        mixed_rows.reshape(BLOCK, HEADS * HEAD_DIM),
        row_max.reshape(BLOCK, HEADS),
        row_sum.reshape(BLOCK, HEADS),
    )


def combine_parts(part_out, part_max, part_sum):
    sources, item_count, head_count = part_max.shape
    part_out = part_out.reshape(sources, item_count, head_count, HEAD_DIM)
    overall = jnp.max(part_max, axis=0)
    factor = jnp.exp(part_max - overall[None])
    weighted = jnp.sum(factor[..., None] * part_out, axis=0)
    normalizer = jnp.sum(factor * part_sum, axis=0)
    return (
        (weighted / normalizer[..., None])
        .reshape(item_count, head_count * HEAD_DIM)
        .astype(jnp.bfloat16)
    )


def migrate_pages(kv_cache, slot_page_after, move_out, move_in):
    slot_ids = jnp.arange(kv_cache.shape[0], dtype=jnp.int32)
    arranged = jnp.where(
        (slot_page_after >= 0)[:, None, None, None], kv_cache, jnp.zeros((), kv_cache.dtype)
    )
    outgoing = kv_cache[jnp.maximum(move_out[0], 0)]
    for offset in range(1, MOVE_WIN + 1):
        arrived = passed_along(outgoing[offset - 1], "pages", offset)
        landing = (slot_ids == move_in[0, offset - 1])[:, None, None, None]
        arranged = jnp.where(landing, arrived[None], arranged)
    return arranged


def local(
    queries, kv_cache, w_out, slot_page_before, slot_page_after, move_out, move_in, positions
):
    owners = lax.axis_size("pages")
    tok_rows = BLOCK // owners
    cache_after = migrate_pages(kv_cache, slot_page_after, move_out, move_in)
    results = []
    for block_index, (cache_rows, slot_table) in enumerate(
        ((kv_cache, slot_page_before), (cache_after, slot_page_after))
    ):
        part_out, part_max, part_sum = block_partials(
            queries[block_index], cache_rows, slot_table, positions[block_index]
        )
        merged = combine_parts(
            lax.all_to_all(
                part_out.reshape(1, owners, tok_rows, D),
                "pages",
                split_axis=1,
                concat_axis=0,
                tiled=True,
            )[:, 0],
            lax.all_to_all(
                part_max.reshape(1, owners, tok_rows, HEADS),
                "pages",
                split_axis=1,
                concat_axis=0,
                tiled=True,
            )[:, 0],
            lax.all_to_all(
                part_sum.reshape(1, owners, tok_rows, HEADS),
                "pages",
                split_axis=1,
                concat_axis=0,
                tiled=True,
            )[:, 0],
        )
        attended = lax.all_to_all(merged, "pages", split_axis=1, concat_axis=0, tiled=True)
        results.append(
            lax.psum_scatter(
                jnp.dot(attended, w_out, preferred_element_type=jnp.float32),
                "pages",
                scatter_dimension=0,
                tiled=True,
            ).astype(jnp.bfloat16)
        )
    return (jnp.stack(results), cache_after)


def solution(mesh):
    in_specs = (
        P(None, "groups", None),
        P(("groups", "pages"), None, None, None),
        P("pages", None),
        P(("groups", "pages")),
        P(("groups", "pages")),
        P(("groups", "pages"), None),
        P(("groups", "pages"), None),
        P(None, "groups"),
    )
    out_specs = (P(None, ("groups", "pages"), None), P(("groups", "pages"), None, None, None))
    return jax.shard_map(local, mesh=mesh, in_specs=in_specs, out_specs=out_specs, check_vma=False)
```

profile of v0, /device:TPU:0, one launch (start us, length us, event | category | flops | bytes accessed | tf_op | source)
XLA Modules:
  0.0 817.3 jit_solution(12786084088419435648)
XLA Ops:
  7.8 7.1 gather_fusion
  17.3 3.1 collective-permute-start
  23.3 18.6 %slice_reduce_fusion.2 = (bf16[8,128,1024]{2,1,0:T(8,128)(2,1)S(1)}, bf16[8,128,1024]{2,1,0:T(8,128)(2,1)}) fusion(bf16[8,128,2,1024]{3,2,1,0:T(2,128)(2,1)S(1)} %copy-done.2), kind=kLoop, calls=%fused_computation.59 | loop fusion | bytes 8388608 | tf_op jit(solution)/shard_map/slice | solution.py:26
  41.9 5.1 slice_bitcast_fusion.1
  47.1 3.1 copy.80
  54.9 4.2 broadcast.127.clone.1
  59.1 126.9 %while.30 = (s32[]{:T(128)}, f32[4,64,8192]{2,1,0:T(8,128)}, f32[4,64,64]{2,1,0:T(8,128)S(1)}, f32[4,64,64]{2,1,0:T(8,128)S(1)}, s32[4,64]{1,0:T(4,128)S(1)}, /*...) while((s32[]{:T(128)}, f32[4,64,8192]{2,1,0:T(8,128)}, ...), condition=%wide.region_3.4_spmd.clone, body=%wide.region_0.3_spmd.clone.sunk | while | flops 2210522112 | bytes 137965520 | solution.py:56
  59.9 5.2 bitcast_reduce_fusion.6
  65.2 5.7 copy-done
  70.9 6.1 convert_reduce_fusion.4
  77.4 8.9 %fusion.58 = f32[64,8,8,128]{3,2,0,1:T(8,128)S(1)} fusion(bf16[1024,8,128]{2,0,1:T(8,128)(2,1)} %get-tuple-element.508, f32[8,64,8,1024]{3,2,1,0:T(8,128)} %copy-done, f32[64,8,8]{2,0,1:T(8,128)S(1)} %get-tuple-element.429, pred[64,1024]{1,0:T(8,128)(4,1)S(1)} %compare_and_fusion.4), kind=kOutput, calls=%fused_computation.16.clone.1 | convolution fusion | flops 1094713344 | bytes 21053440 | tf_op jit(solution)/shard_map/while/body/eval_jaxpr/qhgk,khd->qhgd/dot_general | solution.py:47
  91.5 5.2 bitcast_reduce_fusion.6
  96.8 5.7 copy-done
  102.5 6.1 convert_reduce_fusion.4
  109.1 8.9 %fusion.58 = f32[64,8,8,128]{3,2,0,1:T(8,128)S(1)} fusion(bf16[1024,8,128]{2,0,1:T(8,128)(2,1)} %get-tuple-element.508, f32[8,64,8,1024]{3,2,1,0:T(8,128)} %copy-done, f32[64,8,8]{2,0,1:T(8,128)S(1)} %get-tuple-element.429, pred[64,1024]{1,0:T(8,128)(4,1)S(1)} %compare_and_fusion.4), kind=kOutput, calls=%fused_computation.16.clone.1 | convolution fusion | flops 1094713344 | bytes 21053440 | tf_op jit(solution)/shard_map/while/body/eval_jaxpr/qhgk,khd->qhgd/dot_general | solution.py:47
  123.1 5.2 bitcast_reduce_fusion.6
  128.4 5.7 copy-done
  134.1 6.1 convert_reduce_fusion.4
  140.6 8.9 %fusion.58 = f32[64,8,8,128]{3,2,0,1:T(8,128)S(1)} fusion(bf16[1024,8,128]{2,0,1:T(8,128)(2,1)} %get-tuple-element.508, f32[8,64,8,1024]{3,2,1,0:T(8,128)} %copy-done, f32[64,8,8]{2,0,1:T(8,128)S(1)} %get-tuple-element.429, pred[64,1024]{1,0:T(8,128)(4,1)S(1)} %compare_and_fusion.4), kind=kOutput, calls=%fused_computation.16.clone.1 | convolution fusion | flops 1094713344 | bytes 21053440 | tf_op jit(solution)/shard_map/while/body/eval_jaxpr/qhgk,khd->qhgd/dot_general | solution.py:47
  154.7 5.2 bitcast_reduce_fusion.6
  160.0 5.7 copy-done
  165.7 6.1 convert_reduce_fusion.4
  172.2 8.9 %fusion.58 = f32[64,8,8,128]{3,2,0,1:T(8,128)S(1)} fusion(bf16[1024,8,128]{2,0,1:T(8,128)(2,1)} %get-tuple-element.508, f32[8,64,8,1024]{3,2,1,0:T(8,128)} %copy-done, f32[64,8,8]{2,0,1:T(8,128)S(1)} %get-tuple-element.429, pred[64,1024]{1,0:T(8,128)(4,1)S(1)} %compare_and_fusion.4), kind=kOutput, calls=%fused_computation.16.clone.1 | convolution fusion | flops 1094713344 | bytes 21053440 | tf_op jit(solution)/shard_map/while/body/eval_jaxpr/qhgk,khd->qhgd/dot_general | solution.py:47
  186.8 5.1 all-to-all-start
  193.3 5.5 all-to-all-done
  198.8 3.5 all-to-all-start.2
  203.6 5.4 copy.84
  211.7 6.2 all-to-all-start.1
  218.8 4.6 mul.53
  223.3 9.4 %mul.54 = f32[1,16,16,8192]{3,2,0,1:T(8,128)} reshape(f32[16,16,64,128]{3,2,1,0:T(8,128)} %mul.53) | data formatting | bytes 16777216 | tf_op jit(solution)/shard_map/mul | solution.py:69
  233.1 9.4 %broadcast_select_fusion.4 = bf16[8,128,2,1024]{3,2,1,0:T(2,128)(2,1)S(1)} fusion(pred[8]{0:T(512)(128)(4,1)S(1)} %get-tuple-element.307, pred[8]{0:T(512)(128)(4,1)S(1)} %get-tuple-element.306, pred[8]{0:T(512)(128)(4,1)S(1)} %get-tuple-element.305, pred[8]{0:T(512)(128)(4,1)S(1)} %get-tuple-element.304, bf16[8,128,2,1024]{3,2,1,0:T(2,128)(2,1)} %param.13, ...), kind=kLoop, calls=%fused_computation.55 | loop fusion | flops 10485760 | bytes 10485800 | tf_op jit(solution)/shard_map/jit(_where)/select_n | solution.py:87
  242.5 18.6 %slice_reduce_fusion = (bf16[8,128,1024]{2,1,0:T(8,128)(2,1)S(1)}, bf16[8,128,1024]{2,1,0:T(8,128)(2,1)}) fusion(bf16[8,128,2,1024]{3,2,1,0:T(2,128)(2,1)S(1)} %broadcast_select_fusion.4), kind=kLoop, calls=%fused_computation.56 | loop fusion | bytes 8388608 | tf_op jit(solution)/shard_map/slice | solution.py:26
  267.2 4.2 broadcast.127.clone
  271.4 126.6 %while.31 = (s32[]{:T(128)}, f32[4,64,8192]{2,1,0:T(8,128)}, f32[4,64,64]{2,1,0:T(8,128)S(1)}, f32[4,64,64]{2,1,0:T(8,128)S(1)}, s32[4,64]{1,0:T(4,128)S(1)}, /*...) while((s32[]{:T(128)}, f32[4,64,8192]{2,1,0:T(8,128)}, ...), condition=%wide.region_11.12_spmd.clone, body=%wide.region_8.11_spmd.clone.sunk | while | flops 2210522112 | bytes 137965520 | solution.py:56
  271.9 5.2 bitcast_reduce_fusion.7
  277.2 5.7 copy-done.1
  282.9 6.1 convert_reduce_fusion.5
  289.4 8.9 %fusion.62 = f32[64,8,8,128]{3,2,0,1:T(8,128)S(1)} fusion(bf16[1024,8,128]{2,0,1:T(8,128)(2,1)} %get-tuple-element.475, f32[8,64,8,1024]{3,2,1,0:T(8,128)} %copy-done.1, f32[64,8,8]{2,0,1:T(8,128)S(1)} %get-tuple-element.443, pred[64,1024]{1,0:T(8,128)(4,1)S(1)} %compare_and_fusion.5), kind=kOutput, calls=%fused_computation.38.clone.1 | convolution fusion | flops 1094713344 | bytes 21053440 | tf_op jit(solution)/shard_map/while/body/eval_jaxpr/qhgk,khd->qhgd/dot_general | solution.py:47
  303.5 5.2 bitcast_reduce_fusion.7
  308.8 5.7 copy-done.1
  314.5 6.1 convert_reduce_fusion.5
  321.0 8.9 %fusion.62 = f32[64,8,8,128]{3,2,0,1:T(8,128)S(1)} fusion(bf16[1024,8,128]{2,0,1:T(8,128)(2,1)} %get-tuple-element.475, f32[8,64,8,1024]{3,2,1,0:T(8,128)} %copy-done.1, f32[64,8,8]{2,0,1:T(8,128)S(1)} %get-tuple-element.443, pred[64,1024]{1,0:T(8,128)(4,1)S(1)} %compare_and_fusion.5), kind=kOutput, calls=%fused_computation.38.clone.1 | convolution fusion | flops 1094713344 | bytes 21053440 | tf_op jit(solution)/shard_map/while/body/eval_jaxpr/qhgk,khd->qhgd/dot_general | solution.py:47
  335.2 5.2 bitcast_reduce_fusion.7
  340.4 5.7 copy-done.1
  346.1 6.1 convert_reduce_fusion.5
  352.7 8.9 %fusion.62 = f32[64,8,8,128]{3,2,0,1:T(8,128)S(1)} fusion(bf16[1024,8,128]{2,0,1:T(8,128)(2,1)} %get-tuple-element.475, f32[8,64,8,1024]{3,2,1,0:T(8,128)} %copy-done.1, f32[64,8,8]{2,0,1:T(8,128)S(1)} %get-tuple-element.443, pred[64,1024]{1,0:T(8,128)(4,1)S(1)} %compare_and_fusion.5), kind=kOutput, calls=%fused_computation.38.clone.1 | convolution fusion | flops 1094713344 | bytes 21053440 | tf_op jit(solution)/shard_map/while/body/eval_jaxpr/qhgk,khd->qhgd/dot_general | solution.py:47
  366.7 5.2 bitcast_reduce_fusion.7
  372.0 5.7 copy-done.1
  377.7 6.1 convert_reduce_fusion.5
  384.2 8.9 %fusion.62 = f32[64,8,8,128]{3,2,0,1:T(8,128)S(1)} fusion(bf16[1024,8,128]{2,0,1:T(8,128)(2,1)} %get-tuple-element.475, f32[8,64,8,1024]{3,2,1,0:T(8,128)} %copy-done.1, f32[64,8,8]{2,0,1:T(8,128)S(1)} %get-tuple-element.443, pred[64,1024]{1,0:T(8,128)(4,1)S(1)} %compare_and_fusion.5), kind=kOutput, calls=%fused_computation.38.clone.1 | convolution fusion | flops 1094713344 | bytes 21053440 | tf_op jit(solution)/shard_map/while/body/eval_jaxpr/qhgk,khd->qhgd/dot_general | solution.py:47
  399.5 6.1 all-to-all-start.4
  405.6 6.6 multiply_reduce_fusion.1
  412.6 6.0 all-to-all-start.6
  418.8 6.6 all-to-all-done.6
  425.5 12.6 %all_to_all.86 = bf16[16,16,512]{2,0,1:T(8,128)(2,1)S(1)} all-to-all(bf16[16,16,512]{2,0,1:T(8,128)(2,1)S(1)} %copy.53), channel_id=1, replica_groups=mesh['groups'=2,'pages'=16] {'pages'}, dimensions={1} | all-to-all | bytes 524288 | tf_op jit(solution)/shard_map/all_to_all | solution.py:127
  438.1 4.8 all-to-all-start.5
  442.9 9.0 %fusion.41 = f32[256,8192]{1,0:T(8,128)} fusion(bf16[256,512]{1,0:T(8,128)(2,1)S(1)} %bitcast.262, bf16[512,8192]{1,0:T(8,128)(2,1)} %param.14), kind=kOutput, calls=%fused_computation.96 | convolution fusion | flops 2147483648 | bytes 17039360 | tf_op jit(solution)/shard_map/dot_general | solution.py:130
  453.6 4.9 mul.58
  458.5 9.7 %mul.59 = f32[1,16,16,8192]{3,2,0,1:T(8,128)} reshape(f32[16,16,64,128]{3,2,1,0:T(8,128)} %mul.58) | data formatting | bytes 16777216 | tf_op jit(solution)/shard_map/mul | solution.py:69
  468.5 158.6 %all-to-all-done.5 = f32[1,16,16,8192]{3,2,0,1:T(8,128)} async-done(((f32[1,16,16,8192]{3,2,0,1:T(8,128)}), f32[1,16,16,8192]{3,2,0,1:T(8,128)}, u32[]{:S(2)}, u32[]{:S(2)}) %all-to-all-start.5) | async-done | bytes 8388640 | tf_op jit(solution)/shard_map/all_to_all | solution.py:105
  627.1 7.0 multiply_reduce_fusion
  634.7 62.7 %all_to_all.87 = bf16[16,16,512]{2,0,1:T(8,128)(2,1)S(1)} all-to-all(bf16[16,16,512]{2,0,1:T(8,128)(2,1)S(1)} %copy.61), channel_id=1, replica_groups=mesh['groups'=2,'pages'=16] {'pages'}, dimensions={1} | all-to-all | bytes 524288 | tf_op jit(solution)/shard_map/all_to_all | solution.py:127
  697.4 9.0 %fusion.42 = f32[256,8192]{1,0:T(8,128)} fusion(bf16[256,512]{1,0:T(8,128)(2,1)S(1)} %bitcast.263, bf16[512,8192]{1,0:T(8,128)(2,1)} %param.14), kind=kOutput, calls=%fused_computation.97 | convolution fusion | flops 2147483648 | bytes 17039360 | tf_op jit(solution)/shard_map/dot_general | solution.py:130
  707.5 100.7 %reduce-scatter.5.cloned.1.call-done = f32[16,8192]{1,0:T(8,128)} async-done(((f32[256,8192]{1,0:T(8,128)}), f32[16,8192]{1,0:T(8,128)}) %reduce-scatter.5.cloned.1.call-update) | async-done | bytes 524304 | tf_op jit(solution)/shard_map/reduce_scatter | solution.py:129
  (188 shorter events, 76.0 us)
Async XLA Ops:
  14.9 8.4 %copy-start.2 = (bf16[8,128,2,1024]{3,2,1,0:T(2,128)(2,1)S(1)}, bf16[8,128,2,1024]{3,2,1,0:T(2,128)(2,1)}, u32[]{:S(2)}) copy-start(bf16[8,128,2,1024]{3,2,1,0:T(2,128)(2,1)} %param.13) | copy-start | bytes 12582916
  14.9 27.0 %copy-start.7 = (s32[8]{0:T(128)S(1)}, s32[8]{0:T(128)}, u32[]{:S(2)}) copy-start(s32[8]{0:T(128)} %param.15) | copy-start | bytes 100
  17.3 215.7 %collective-permute-start = (bf16[128,2,1024]{2,1,0:T(2,128)(2,1)}, bf16[128,2,1024]{2,1,0:T(2,128)(2,1)}, u32[]{:S(2)}, u32[]{:S(2)}) collective-permute-start(bf16[128,2,1024]{2,1,0:T(2,128)(2,1)} %get-tuple-element.296), channel_id=1, source_target_pairs={{12,0},{13,1},{14,2},{15,3},{0,4},{1,5},{2,6},{3,7},{4,8},{5,9},{6... | collective-permute-start | bytes 1572872 | tf_op jit(solution)/shard_map/ppermute | solution.py:19
  20.4 212.7 %collective-permute-start.1 = (bf16[128,2,1024]{2,1,0:T(2,128)(2,1)}, bf16[128,2,1024]{2,1,0:T(2,128)(2,1)}, u32[]{:S(2)}, u32[]{:S(2)}) collective-permute-start(bf16[128,2,1024]{2,1,0:T(2,128)(2,1)} %get-tuple-element.298), channel_id=1, source_target_pairs={{13,0},{14,1},{15,2},{0,3},{1,4},{2,5},{3,6},{4,7},{5,8},{6,9},{7,... | collective-permute-start | bytes 1572872 | tf_op jit(solution)/shard_map/ppermute | solution.py:19
  21.0 212.0 %collective-permute-start.2 = (bf16[128,2,1024]{2,1,0:T(2,128)(2,1)}, bf16[128,2,1024]{2,1,0:T(2,128)(2,1)}, u32[]{:S(2)}, u32[]{:S(2)}) collective-permute-start(bf16[128,2,1024]{2,1,0:T(2,128)(2,1)} %get-tuple-element.297), channel_id=1, source_target_pairs={{14,0},{15,1},{0,2},{1,3},{2,4},{3,5},{4,6},{5,7},{6,8},{7,9},{8,1... | collective-permute-start | bytes 1572872 | tf_op jit(solution)/shard_map/ppermute | solution.py:19
  22.6 210.5 %collective-permute-start.3 = (bf16[128,2,1024]{2,1,0:T(2,128)(2,1)}, bf16[128,2,1024]{2,1,0:T(2,128)(2,1)}, u32[]{:S(2)}, u32[]{:S(2)}) collective-permute-start(bf16[128,2,1024]{2,1,0:T(2,128)(2,1)} %get-tuple-element.299), channel_id=1, source_target_pairs={{15,0},{0,1},{1,2},{2,3},{3,4},{4,5},{5,6},{6,7},{7,8},{8,9},{9,10... | collective-permute-start | bytes 1572872 | tf_op jit(solution)/shard_map/ppermute | solution.py:19
  41.9 5.1 copy-start.6
  47.0 3.1 copy-start.4
  59.1 132.8 %copy-start.8 = (s32[8]{0:T(128)S(1)}, s32[8]{0:T(128)}, u32[]{:S(2)}) copy-start(s32[8]{0:T(128)} %param.16) | copy-start | bytes 100
  59.1 133.6 %copy-start.5 = (s32[1,4]{1,0:T(1,128)S(1)}, s32[1,4]{1,0:T(1,128)}, u32[]{:S(2)}) copy-start(s32[1,4]{1,0:T(1,128)} %param.18) | copy-start | bytes 52
  65.2 5.7 copy-start
  96.8 5.7 copy-start
  128.3 5.7 copy-start
  160.0 5.7 copy-start
  186.8 12.0 %all-to-all-start = ((f32[16,1,1024]{2,1,0:T(1,128)}), f32[16,1,1024]{2,1,0:T(1,128)S(1)}, u32[]{:S(2)}, u32[]{:S(2)}) async-start(f32[16,1,1024]{2,1,0:T(1,128)} %reshape.268), calls=%async_computation | async-start | bytes 131072 | tf_op jit(solution)/shard_map/all_to_all | solution.py:112
  198.8 12.9 %all-to-all-start.2 = ((f32[16,1,1024]{2,1,0:T(1,128)}), f32[16,1,1024]{2,1,0:T(1,128)S(1)}, u32[]{:S(2)}, u32[]{:S(2)}) async-start(f32[16,1,1024]{2,1,0:T(1,128)} %reshape.270), calls=%async_computation.2 | async-start | bytes 131072 | tf_op jit(solution)/shard_map/all_to_all | solution.py:119
  211.7 187.9 %all-to-all-start.1 = ((f32[1,16,16,8192]{3,2,0,1:T(8,128)}), f32[1,16,16,8192]{3,2,0,1:T(8,128)}, u32[]{:S(2)}, u32[]{:S(2)}) async-start(f32[1,16,16,8192]{3,2,0,1:T(8,128)} %bitcast.245), calls=%async_computation.1 | async-start | bytes 16777216 | tf_op jit(solution)/shard_map/all_to_all | solution.py:105
  242.5 20.8 %copy-start.3 = (bf16[8,128,2,1024]{3,2,1,0:T(2,128)(2,1)}, bf16[8,128,2,1024]{3,2,1,0:T(2,128)(2,1)S(1)}, u32[]{:S(2)}) copy-start(bf16[8,128,2,1024]{3,2,1,0:T(2,128)(2,1)S(1)} %broadcast_select_fusion.4) | copy-start | bytes 12582916
  277.2 5.7 copy-start.1
  308.8 5.7 copy-start.1
  340.4 5.7 copy-start.1
  372.0 5.7 copy-start.1
  399.5 13.0 %all-to-all-start.4 = ((f32[16,1,1024]{2,1,0:T(1,128)}), f32[16,1,1024]{2,1,0:T(1,128)S(1)}, u32[]{:S(2)}, u32[]{:S(2)}) async-start(f32[16,1,1024]{2,1,0:T(1,128)} %reshape.264), calls=%async_computation.5 | async-start | bytes 131072 | tf_op jit(solution)/shard_map/all_to_all | solution.py:112
  412.6 12.9 %all-to-all-start.6 = ((f32[16,1,1024]{2,1,0:T(1,128)}), f32[16,1,1024]{2,1,0:T(1,128)S(1)}, u32[]{:S(2)}, u32[]{:S(2)}) async-start(f32[16,1,1024]{2,1,0:T(1,128)} %reshape.266), calls=%async_computation.7 | async-start | bytes 131072 | tf_op jit(solution)/shard_map/all_to_all | solution.py:119
  438.1 189.1 %all-to-all-start.5 = ((f32[1,16,16,8192]{3,2,0,1:T(8,128)}), f32[1,16,16,8192]{3,2,0,1:T(8,128)}, u32[]{:S(2)}, u32[]{:S(2)}) async-start(f32[1,16,16,8192]{3,2,0,1:T(8,128)} %bitcast.244), calls=%async_computation.6 | async-start | bytes 16777216 | tf_op jit(solution)/shard_map/all_to_all | solution.py:105
  442.9 263.6 %reduce-scatter.3.cloned.1.call-start = ((), (), s32[]{:S(2)}) async-start(), calls=%async_computation.10 | async-start | bytes 8912896 | tf_op jit(solution)/shard_map/reduce_scatter | solution.py:129
  451.9 356.3 %reduce-scatter.5.cloned.1.call-start = ((), (), s32[]{:S(2)}) async-start(), calls=%async_computation.11 | async-start | bytes 8912896 | tf_op jit(solution)/shard_map/reduce_scatter | solution.py:129
Sparse Core Ops, SparseCore 0:
  452.0 206.1 reduce-scatter.2
  706.5 101.6 reduce-scatter.4
where the time goes:
time: 826 us; the launch traced here: 817 us
  waiting for transfers between devices  271 us (33%)
  local copies, waits for them, and re-layouts  203 us (25%)
  matrix products  131 us (16%)
  other arithmetic  82.8 us (10%)
  blocking collectives  75.3 us (9%)
  starting transfers between devices  37.8 us (5%)
  between operations  14.7 us (2%)
    all_to_all x2, waiting for transfers between devices, local(): lax.all_to_all(part_out.reshape(1, owners, tok_rows, D), 'pages', split_a...  159 us
    reduce_scatter x2, waiting for transfers between devices, local(): lax.psum_scatter(jnp.dot(attended, w_out, preferred_element_type=jnp.floa...  101 us
    all_to_all x2, blocking collectives, local(): lax.all_to_all(merged, 'pages', split_axis=1, concat_axis=0, tiled=True)  75.3 us
    dot_general x8, matrix products, one_block(): jnp.einsum('qhgk,khd->qhgd', weights, value_rows, preferred_element_type=...  71.5 us
    reduce_sum x8, other arithmetic, one_block(): row_sum = jnp.sum(weights, axis=-1, dtype=jnp.float32)  49 us
    while x16, local copies, waits for them, and re-layouts  45.6 us
    dot_general x8, matrix products, one_block(): jnp.einsum('qhgd,khd->qhgk', query_block, key_rows, preferred_element_typ...  41.9 us
    slice x2, local copies, waits for them, and re-layouts, block_partials(): value_rows = cache_rows[:, :, 1, :].reshape(key_count, KV_HEADS, HEAD_DIM)  37.2 us
  transfers between devices with their start and end apart: 12, of which 4 were waited for; matrix products, arithmetic and copies ran while one was open for 44% of the time, Pallas kernels for 0%

commit v1 on v0

--- a/solution.py
+++ b/solution.py
@@ -11,6 +11,29 @@
 BLOCK = 256
 MOVE_WIN = 4
 floor_score = -1e30
+
+
+def cut_along(value, dim, length):
+    shape = value.shape
+    blocks = value.reshape(*shape[:dim], length, shape[dim] // length, *shape[dim + 1 :])
+    return jnp.moveaxis(blocks, dim, 0)
+
+
+def in_order(blocks, dim):
+    blocks = jnp.moveaxis(blocks, 0, dim)
+    dims = blocks.shape
+    return blocks.reshape(*dims[:dim], dims[dim] * dims[dim + 1], *dims[dim + 2 :])
+
+
+def pairwise_exchange(shard, axis, split_dim, concat_dim):
+    size, index = (lax.axis_size(axis), lax.axis_index(axis))
+    parts = cut_along(shard, split_dim, size)
+    outs = [parts[index]]
+    for step in range(1, size):
+        sent = parts[index ^ step]
+        outs.append(lax.ppermute(sent, axis, [(i, i ^ step) for i in range(size)]))
+    parts = jnp.stack(outs)[index ^ jnp.arange(size)]
+    return in_order(parts, concat_dim)
 
 
 def passed_along(block, axis, distance):
@@ -102,13 +125,7 @@
             queries[block_index], cache_rows, slot_table, positions[block_index]
         )
         merged = combine_parts(
-            lax.all_to_all(
-                part_out.reshape(1, owners, tok_rows, D),
-                "pages",
-                split_axis=1,
-                concat_axis=0,
-                tiled=True,
-            )[:, 0],
+            pairwise_exchange(part_out.reshape(1, owners, tok_rows, D), "pages", 1, 0)[:, 0],
             lax.all_to_all(
                 part_max.reshape(1, owners, tok_rows, HEADS),
                 "pages",

time: 826 us -> 1100 us (1.33)
  starting transfers between devices: 37.8 us -> 163 us
  waiting for transfers between devices: 271 us -> 387 us
  local copies, waits for them, and re-layouts: 203 us -> 247 us
    ppermute x0 -> x30, waiting for transfers between devices: none -> 272 us  [pairwise_exchange(): outs.append(lax.ppermute(sent, axis, [(i, i ^ step) for i in range(size)]))]
    all_to_all x2 -> x1, waiting for transfers between devices: 159 us -> 0.01 us  [local(): lax.all_to_all(merged, 'pages', split_axis=1, concat_axis=0, tiled=True)]
    ppermute x0 -> x30, starting transfers between devices: none -> 47.6 us  [pairwise_exchange(): outs.append(lax.ppermute(sent, axis, [(i, i ^ step) for i in range(size)]))]
    ppermute x4, starting transfers between devices: 5.98 us -> 51.3 us  [passed_along(): return lax.ppermute(block, axis, route)]
    unnamed x35 -> x75, local copies, waits for them, and re-layouts: 28.4 us -> 69.7 us
    all_to_all x2, starting transfers between devices: 11.2 us -> 51.5 us  [local(): lax.all_to_all(part_max.reshape(1, owners, tok_rows, HEADS), 'pages', spl...]
    mul x4 -> x0, local copies, waits for them, and re-layouts: 28.6 us -> none  [combine_parts(): weighted = jnp.sum(factor[..., None] * part_out, axis=0)]
    gather x0 -> x2, local copies, waits for them, and re-layouts: none -> 15.5 us  [pairwise_exchange(): parts = jnp.stack(outs)[index ^ jnp.arange(size)]]
  transfers between devices with their start and end apart: 12 -> 41, of which waited for: 4 -> 14; matrix products, arithmetic and copies ran while one was open for 44% -> 11% of each run, Pallas kernels for 0% -> 0%
where the time goes in v1:
time: 1100 us
  waiting for transfers between devices  387 us (35%)
  local copies, waits for them, and re-layouts  247 us (22%)
  starting transfers between devices  163 us (15%)
  matrix products  131 us (12%)
  other arithmetic  79 us (7%)
  blocking collectives  72 us (7%)
  between operations  14.7 us (1%)
    ppermute x30, waiting for transfers between devices, pairwise_exchange(): outs.append(lax.ppermute(sent, axis, [(i, i ^ step) for i in range(size)]))  272 us
    reduce_scatter x2, waiting for transfers between devices, local(): lax.psum_scatter(jnp.dot(attended, w_out, preferred_element_type=jnp.floa...  101 us
    all_to_all x1, blocking collectives, local(): lax.all_to_all(merged, 'pages', split_axis=1, concat_axis=0, tiled=True)  72 us
    dot_general x8, matrix products, one_block(): jnp.einsum('qhgk,khd->qhgd', weights, value_rows, preferred_element_type=...  71.5 us
    unnamed x75, local copies, waits for them, and re-layouts  69.7 us
    all_to_all x2, starting transfers between devices, local(): lax.all_to_all(part_max.reshape(1, owners, tok_rows, HEADS), 'pages', spl...  51.5 us
    ppermute x4, starting transfers between devices, passed_along(): return lax.ppermute(block, axis, route)  51.3 us
    reduce_sum x8, other arithmetic, one_block(): row_sum = jnp.sum(weights, axis=-1, dtype=jnp.float32)  49 us
  transfers between devices with their start and end apart: 41, of which 14 were waited for; matrix products, arithmetic and copies ran while one was open for 11% of the time, Pallas kernels for 0%

profile of v1, /device:TPU:0, one launch (start us, length us, event | category | flops | bytes accessed | tf_op | source)
XLA Modules:
  0.0 1095.7 jit_solution(14638407864464385658)
XLA Ops:
  16.8 18.6 %slice_reduce_fusion.2 = (bf16[8,128,1024]{2,1,0:T(8,128)(2,1)S(1)}, bf16[8,128,1024]{2,1,0:T(8,128)(2,1)}) fusion(bf16[8,128,2,1024]{3,2,1,0:T(2,128)(2,1)S(1)} %copy-done.2), kind=kLoop, calls=%fused_computation.63 | loop fusion | bytes 8388608 | tf_op jit(solution)/shard_map/slice | solution.py:49
  46.0 126.8 %while.30 = (s32[]{:T(128)}, f32[4,64,8192]{2,1,0:T(8,128)}, f32[4,64,64]{2,1,0:T(8,128)S(1)}, f32[4,64,64]{2,1,0:T(8,128)S(1)}, s32[4,64]{1,0:T(4,128)S(1)}, /*...) while((s32[]{:T(128)}, f32[4,64,8192]{2,1,0:T(8,128)}, ...), condition=%wide.region_3.4_spmd.clone, body=%wide.region_0.3_spmd.clone.sunk | while | flops 2210522112 | bytes 137965520 | solution.py:79
  46.4 5.2 bitcast_reduce_fusion.6
  51.7 5.7 copy-done
  57.4 6.1 convert_reduce_fusion.4
  64.0 8.9 fusion.59
  83.3 5.7 copy-done
  89.1 6.1 convert_reduce_fusion.4
  95.6 8.9 fusion.59
  109.7 5.2 bitcast_reduce_fusion.6
  114.9 5.7 copy-done
  120.7 6.1 convert_reduce_fusion.4
  127.2 8.9 fusion.59
  141.3 5.2 bitcast_reduce_fusion.6
  146.6 5.7 copy-done
  152.3 6.1 convert_reduce_fusion.4
  158.9 8.9 fusion.59
  172.7 6.7 dynamic-slice_bitcast_fusion.15
  185.2 6.1 all-to-all-start
  192.0 7.1 gather_fusion.1
  204.8 7.7 all-to-all-done
  216.3 5.5 copy.84
  241.9 16.2 %collective-permute-done.5 = f32[1,1,16,8192]{3,2,1,0:T(8,128)S(1)} collective-permute-done((f32[1,1,16,8192]{3,2,1,0:T(8,128)}, f32[1,1,16,8192]{3,2,1,0:T(8,128)S(1)}, u32[]{:S(2)}, u32[]{:S(2)}) %collective-permute-start.5) | collective-permute-done | bytes 524320 | tf_op jit(solution)/shard_map/ppermute | solution.py:34
  259.0 9.2 collective-permute-done.6
  273.8 51.8 %collective-permute-done.8 = f32[1,1,16,8192]{3,2,1,0:T(8,128)S(1)} collective-permute-done((f32[1,1,16,8192]{3,2,1,0:T(8,128)}, f32[1,1,16,8192]{3,2,1,0:T(8,128)S(1)}, u32[]{:S(2)}, u32[]{:S(2)}) %collective-permute-start.8) | collective-permute-done | bytes 524320 | tf_op jit(solution)/shard_map/ppermute | solution.py:34
  331.2 18.9 %collective-permute-done.9 = f32[1,1,16,8192]{3,2,1,0:T(8,128)S(1)} collective-permute-done((f32[1,1,16,8192]{3,2,1,0:T(8,128)}, f32[1,1,16,8192]{3,2,1,0:T(8,128)S(1)}, u32[]{:S(2)}, u32[]{:S(2)}) %collective-permute-start.9) | collective-permute-done | bytes 524320 | tf_op jit(solution)/shard_map/ppermute | solution.py:34
  353.4 18.6 %collective-permute-done.10 = f32[1,1,16,8192]{3,2,1,0:T(8,128)S(1)} collective-permute-done((f32[1,1,16,8192]{3,2,1,0:T(8,128)}, f32[1,1,16,8192]{3,2,1,0:T(8,128)S(1)}, u32[]{:S(2)}, u32[]{:S(2)}) %collective-permute-start.10) | collective-permute-done | bytes 524320 | tf_op jit(solution)/shard_map/ppermute | solution.py:34
  374.3 26.9 %collective-permute-start.17 = (bf16[128,2,1024]{2,1,0:T(2,128)(2,1)}, bf16[128,2,1024]{2,1,0:T(2,128)(2,1)S(1)}, u32[]{:S(2)}, u32[]{:S(2)}) collective-permute-start(bf16[128,2,1024]{2,1,0:T(2,128)(2,1)} %get-tuple-element.329), channel_id=1, source_target_pairs={{14,0},{15,1},{0,2},{1,3},{2,4},{3,5},{4,6},{5,7},{6,8},{7,9},{8,1... | collective-permute-start | bytes 1572872 | tf_op jit(solution)/shard_map/ppermute | solution.py:42
  402.0 23.7 %collective-permute-start.18 = (bf16[128,2,1024]{2,1,0:T(2,128)(2,1)}, bf16[128,2,1024]{2,1,0:T(2,128)(2,1)S(1)}, u32[]{:S(2)}, u32[]{:S(2)}) collective-permute-start(bf16[128,2,1024]{2,1,0:T(2,128)(2,1)} %get-tuple-element.331), channel_id=1, source_target_pairs={{15,0},{0,1},{1,2},{2,3},{3,4},{4,5},{5,6},{6,7},{7,8},{8,9},{9,10... | collective-permute-start | bytes 1572872 | tf_op jit(solution)/shard_map/ppermute | solution.py:42
  427.4 7.7 gather_fusion
  435.2 8.4 copy.83
  443.6 8.9 broadcast_select_fusion.4
  452.5 18.6 %slice_reduce_fusion = (bf16[8,128,1024]{2,1,0:T(8,128)(2,1)S(1)}, bf16[8,128,1024]{2,1,0:T(8,128)(2,1)}) fusion(bf16[8,128,2,1024]{3,2,1,0:T(2,128)(2,1)S(1)} %broadcast_select_fusion.4), kind=kLoop, calls=%fused_computation.60 | loop fusion | bytes 8388608 | tf_op jit(solution)/shard_map/slice | solution.py:49
  481.5 127.0 %while.31 = (s32[]{:T(128)}, f32[4,64,8192]{2,1,0:T(8,128)}, f32[4,64,64]{2,1,0:T(8,128)S(1)}, f32[4,64,64]{2,1,0:T(8,128)S(1)}, s32[4,64]{1,0:T(4,128)S(1)}, /*...) while((s32[]{:T(128)}, f32[4,64,8192]{2,1,0:T(8,128)}, ...), condition=%wide.region_11.12_spmd.clone, body=%wide.region_8.11_spmd.clone.sunk | while | flops 2210522112 | bytes 137965520 | solution.py:79
  482.2 5.2 bitcast_reduce_fusion.7
  487.5 5.7 copy-done.1
  493.2 6.1 convert_reduce_fusion.5
  499.8 8.9 fusion.63
  513.9 5.2 bitcast_reduce_fusion.7
  519.2 5.7 copy-done.1
  524.9 6.1 convert_reduce_fusion.5
  531.5 8.9 fusion.63
  545.5 5.2 bitcast_reduce_fusion.7
  550.8 5.7 copy-done.1
  556.5 6.1 convert_reduce_fusion.5
  563.1 8.9 fusion.63
  577.2 5.2 bitcast_reduce_fusion.7
  582.5 5.7 copy-done.1
  588.2 6.1 convert_reduce_fusion.5
  594.7 8.9 fusion.63
  609.3 45.4 %all-to-all-start.3 = ((f32[16,1,1024]{2,1,0:T(1,128)}), f32[16,1,1024]{2,1,0:T(1,128)S(1)}, u32[]{:S(2)}, u32[]{:S(2)}) async-start(f32[16,1,1024]{2,1,0:T(1,128)} %reshape.320), calls=%async_computation.4 | async-start | bytes 131072 | tf_op jit(solution)/shard_map/all_to_all | solution.py:129
  654.7 5.3 fusion.33
  668.0 5.7 all-to-all-done.4
  677.4 6.8 dynamic-slice_bitcast_fusion
  689.9 9.0 fusion.42
  703.3 6.2 collective-permute-done.21
  718.7 44.3 %collective-permute-done.24 = f32[1,1,16,8192]{3,2,1,0:T(8,128)S(1)} collective-permute-done((f32[1,1,16,8192]{3,2,1,0:T(8,128)}, f32[1,1,16,8192]{3,2,1,0:T(8,128)S(1)}, u32[]{:S(2)}, u32[]{:S(2)}) %collective-permute-start.24) | collective-permute-done | bytes 524320 | tf_op jit(solution)/shard_map/ppermute | solution.py:34
  763.8 14.5 %collective-permute-done.25 = f32[1,1,16,8192]{3,2,1,0:T(8,128)S(1)} collective-permute-done((f32[1,1,16,8192]{3,2,1,0:T(8,128)}, f32[1,1,16,8192]{3,2,1,0:T(8,128)S(1)}, u32[]{:S(2)}, u32[]{:S(2)}) %collective-permute-start.25) | collective-permute-done | bytes 524320 | tf_op jit(solution)/shard_map/ppermute | solution.py:34
  786.2 72.2 %collective-permute-done.28 = f32[1,1,16,8192]{3,2,1,0:T(8,128)S(1)} collective-permute-done((f32[1,1,16,8192]{3,2,1,0:T(8,128)}, f32[1,1,16,8192]{3,2,1,0:T(8,128)S(1)}, u32[]{:S(2)}, u32[]{:S(2)}) %collective-permute-start.28) | collective-permute-done | bytes 524320 | tf_op jit(solution)/shard_map/ppermute | solution.py:34
  863.3 20.3 %collective-permute-done.29 = f32[1,1,16,8192]{3,2,1,0:T(8,128)S(1)} collective-permute-done((f32[1,1,16,8192]{3,2,1,0:T(8,128)}, f32[1,1,16,8192]{3,2,1,0:T(8,128)S(1)}, u32[]{:S(2)}, u32[]{:S(2)}) %collective-permute-start.29) | collective-permute-done | bytes 524320 | tf_op jit(solution)/shard_map/ppermute | solution.py:34
  887.9 7.8 gather_fusion.2
  903.8 72.0 %all_to_all.68 = bf16[16,16,512]{2,0,1:T(8,128)(2,1)S(1)} all-to-all(bf16[16,16,512]{2,0,1:T(8,128)(2,1)S(1)} %copy.61), channel_id=1, replica_groups=mesh['groups'=2,'pages'=16] {'pages'}, dimensions={1} | all-to-all | bytes 524288 | tf_op jit(solution)/shard_map/all_to_all | solution.py:144
  975.8 9.1 fusion.43
  986.0 100.7 %reduce-scatter.5.cloned.1.call-done = f32[16,8192]{1,0:T(8,128)} async-done(((f32[256,8192]{1,0:T(8,128)}), f32[16,8192]{1,0:T(8,128)}) %reduce-scatter.5.cloned.1.call-update) | async-done | bytes 524304 | tf_op jit(solution)/shard_map/reduce_scatter | solution.py:146
  (287 shorter events, 196.9 us)
Async XLA Ops:
  13.7 3.2 copy-start.2
  35.4 6.2 copy-start.12
  51.7 5.7 copy-start
  83.3 5.7 copy-start
  114.9 5.7 copy-start
  146.6 5.7 copy-start
  172.7 18.5 %copy-start.13 = (s32[8]{0:T(128)S(1)}, s32[8]{0:T(128)}, u32[]{:S(2)}) copy-start(s32[8]{0:T(128)} %param.16) | copy-start | bytes 100
  172.7 18.6 %copy-start.10 = (s32[1,4]{1,0:T(1,128)S(1)}, s32[1,4]{1,0:T(1,128)}, u32[]{:S(2)}) copy-start(s32[1,4]{1,0:T(1,128)} %param.18) | copy-start | bytes 52
  172.7 19.3 %copy-start.14 = (s32[1,4]{1,0:T(1,128)S(1)}, s32[1,4]{1,0:T(1,128)}, u32[]{:S(2)}) copy-start(s32[1,4]{1,0:T(1,128)} %param.17) | copy-start | bytes 52
  179.4 46.1 %collective-permute-start = (f32[1,1,16,8192]{3,2,1,0:T(8,128)}, f32[1,1,16,8192]{3,2,1,0:T(8,128)}, u32[]{:S(2)}, u32[]{:S(2)}) collective-permute-start(f32[1,1,16,8192]{3,2,1,0:T(8,128)} %get-tuple-element.308), channel_id=1, source_target_pairs={{0,1},{1,0},{2,3},{3,2},{4,5},{5,4},{6,7},{7,6},{8,9},{9,8},{10,11... | collective-permute-start | bytes 1572872 | tf_op jit(solution)/shard_map/ppermute | solution.py:34
  180.0 50.2 %collective-permute-start.1 = (f32[1,1,16,8192]{3,2,1,0:T(8,128)}, f32[1,1,16,8192]{3,2,1,0:T(8,128)}, u32[]{:S(2)}, u32[]{:S(2)}) collective-permute-start(f32[1,1,16,8192]{3,2,1,0:T(8,128)} %get-tuple-element.307), channel_id=1, source_target_pairs={{0,2},{1,3},{2,0},{3,1},{4,6},{5,7},{6,4},{7,5},{8,10},{9,11},{10,... | collective-permute-start | bytes 1572872 | tf_op jit(solution)/shard_map/ppermute | solution.py:34
  182.6 49.5 %collective-permute-start.2 = (f32[1,1,16,8192]{3,2,1,0:T(8,128)}, f32[1,1,16,8192]{3,2,1,0:T(8,128)}, u32[]{:S(2)}, u32[]{:S(2)}) collective-permute-start(f32[1,1,16,8192]{3,2,1,0:T(8,128)} %get-tuple-element.306), channel_id=1, source_target_pairs={{0,3},{1,2},{2,1},{3,0},{4,7},{5,6},{6,5},{7,4},{8,11},{9,10},{10,... | collective-permute-start | bytes 1572872 | tf_op jit(solution)/shard_map/ppermute | solution.py:34
  182.6 53.8 %collective-permute-start.3 = (f32[1,1,16,8192]{3,2,1,0:T(8,128)}, f32[1,1,16,8192]{3,2,1,0:T(8,128)S(1)}, u32[]{:S(2)}, u32[]{:S(2)}) collective-permute-start(f32[1,1,16,8192]{3,2,1,0:T(8,128)} %get-tuple-element.305), channel_id=1, source_target_pairs={{0,4},{1,5},{2,6},{3,7},{4,0},{5,1},{6,2},{7,3},{8,12},{9,13},{10,... | collective-permute-start | bytes 1572872 | tf_op jit(solution)/shard_map/ppermute | solution.py:34
  184.4 53.1 %collective-permute-start.4 = (f32[1,1,16,8192]{3,2,1,0:T(8,128)}, f32[1,1,16,8192]{3,2,1,0:T(8,128)S(1)}, u32[]{:S(2)}, u32[]{:S(2)}) collective-permute-start(f32[1,1,16,8192]{3,2,1,0:T(8,128)} %get-tuple-element.304), channel_id=1, source_target_pairs={{0,5},{1,4},{2,7},{3,6},{4,1},{5,0},{6,3},{7,2},{8,13},{9,12},{10,... | collective-permute-start | bytes 1572872 | tf_op jit(solution)/shard_map/ppermute | solution.py:34
  185.2 27.4 %all-to-all-start = ((f32[16,1,1024]{2,1,0:T(1,128)}), f32[16,1,1024]{2,1,0:T(1,128)S(1)}, u32[]{:S(2)}, u32[]{:S(2)}) async-start(f32[16,1,1024]{2,1,0:T(1,128)} %reshape.324), calls=%async_computation | async-start | bytes 131072 | tf_op jit(solution)/shard_map/all_to_all | solution.py:129
  201.5 66.8 %copy-start.8 = (f32[1,1,16,8192]{3,2,1,0:T(8,128)S(1)}, f32[1,1,16,8192]{3,2,1,0:T(8,128)}, u32[]{:S(2)}) copy-start(f32[1,1,16,8192]{3,2,1,0:T(8,128)} %get-tuple-element.297) | copy-start | bytes 1572868
  212.5 10.8 all-to-all-start.1
  216.2 54.2 %copy-start.7 = (f32[1,1,16,8192]{3,2,1,0:T(8,128)S(1)}, f32[1,1,16,8192]{3,2,1,0:T(8,128)}, u32[]{:S(2)}) copy-start(f32[1,1,16,8192]{3,2,1,0:T(8,128)} %get-tuple-element.296) | copy-start | bytes 1572868
  216.3 109.4 %copy-start.6 = (f32[1,1,16,8192]{3,2,1,0:T(8,128)S(1)}, f32[1,1,16,8192]{3,2,1,0:T(8,128)}, u32[]{:S(2)}) copy-start(f32[1,1,16,8192]{3,2,1,0:T(8,128)} %get-tuple-element.295) | copy-start | bytes 1572868
  221.9 205.6 %copy-start.11 = (s32[1024]{0:T(1024)}, s32[1024]{0:T(1024)S(1)}, u32[]{:S(2)}) copy-start(s32[1024]{0:T(1024)S(1)} %pad_clamp_fusion.1) | copy-start | bytes 12292
  225.5 32.7 %collective-permute-start.5 = (f32[1,1,16,8192]{3,2,1,0:T(8,128)}, f32[1,1,16,8192]{3,2,1,0:T(8,128)S(1)}, u32[]{:S(2)}, u32[]{:S(2)}) collective-permute-start(f32[1,1,16,8192]{3,2,1,0:T(8,128)} %get-tuple-element.303), channel_id=1, source_target_pairs={{0,6},{1,7},{2,4},{3,5},{4,2},{5,3},{6,0},{7,1},{8,14},{9,15},{10,... | collective-permute-start | bytes 1572872 | tf_op jit(solution)/shard_map/ppermute | solution.py:34
  230.2 38.0 %collective-permute-start.6 = (f32[1,1,16,8192]{3,2,1,0:T(8,128)}, f32[1,1,16,8192]{3,2,1,0:T(8,128)S(1)}, u32[]{:S(2)}, u32[]{:S(2)}) collective-permute-start(f32[1,1,16,8192]{3,2,1,0:T(8,128)} %get-tuple-element.302), channel_id=1, source_target_pairs={{0,7},{1,6},{2,5},{3,4},{4,3},{5,2},{6,1},{7,0},{8,15},{9,14},{10,... | collective-permute-start | bytes 1572872 | tf_op jit(solution)/shard_map/ppermute | solution.py:34
  232.1 38.3 %collective-permute-start.7 = (f32[1,1,16,8192]{3,2,1,0:T(8,128)}, f32[1,1,16,8192]{3,2,1,0:T(8,128)S(1)}, u32[]{:S(2)}, u32[]{:S(2)}) collective-permute-start(f32[1,1,16,8192]{3,2,1,0:T(8,128)} %get-tuple-element.301), channel_id=1, source_target_pairs={{0,8},{1,9},{2,10},{3,11},{4,12},{5,13},{6,14},{7,15},{8,0},{9,1},... | collective-permute-start | bytes 1572872 | tf_op jit(solution)/shard_map/ppermute | solution.py:34
  236.4 89.2 %collective-permute-start.8 = (f32[1,1,16,8192]{3,2,1,0:T(8,128)}, f32[1,1,16,8192]{3,2,1,0:T(8,128)S(1)}, u32[]{:S(2)}, u32[]{:S(2)}) collective-permute-start(f32[1,1,16,8192]{3,2,1,0:T(8,128)} %get-tuple-element.300), channel_id=1, source_target_pairs={{0,9},{1,8},{2,11},{3,10},{4,13},{5,12},{6,15},{7,14},{8,1},{9,0},... | collective-permute-start | bytes 1572872 | tf_op jit(solution)/shard_map/ppermute | solution.py:34
  237.5 112.5 %collective-permute-start.9 = (f32[1,1,16,8192]{3,2,1,0:T(8,128)}, f32[1,1,16,8192]{3,2,1,0:T(8,128)S(1)}, u32[]{:S(2)}, u32[]{:S(2)}) collective-permute-start(f32[1,1,16,8192]{3,2,1,0:T(8,128)} %get-tuple-element.299), channel_id=1, source_target_pairs={{0,10},{1,11},{2,8},{3,9},{4,14},{5,15},{6,12},{7,13},{8,2},{9,3},... | collective-permute-start | bytes 1572872 | tf_op jit(solution)/shard_map/ppermute | solution.py:34
  258.2 113.8 %collective-permute-start.10 = (f32[1,1,16,8192]{3,2,1,0:T(8,128)}, f32[1,1,16,8192]{3,2,1,0:T(8,128)S(1)}, u32[]{:S(2)}, u32[]{:S(2)}) collective-permute-start(f32[1,1,16,8192]{3,2,1,0:T(8,128)} %get-tuple-element.298), channel_id=1, source_target_pairs={{0,11},{1,10},{2,9},{3,8},{4,15},{5,14},{6,13},{7,12},{8,3},{9,2},... | collective-permute-start | bytes 1572872 | tf_op jit(solution)/shard_map/ppermute | solution.py:34
  268.2 104.9 %collective-permute-start.11 = (f32[1,1,16,8192]{3,2,1,0:T(8,128)S(1)}, f32[1,1,16,8192]{3,2,1,0:T(8,128)S(1)}, u32[]{:S(2)}, u32[]{:S(2)}) collective-permute-start(f32[1,1,16,8192]{3,2,1,0:T(8,128)S(1)} %copy-done.8), channel_id=1, source_target_pairs={{0,12},{1,13},{2,14},{3,15},{4,8},{5,9},{6,10},{7,11},{8,4},{9,5},... | collective-permute-start | bytes 1572872 | tf_op jit(solution)/shard_map/ppermute | solution.py:34
  270.4 103.8 %collective-permute-start.12 = (f32[1,1,16,8192]{3,2,1,0:T(8,128)S(1)}, f32[1,1,16,8192]{3,2,1,0:T(8,128)S(1)}, u32[]{:S(2)}, u32[]{:S(2)}) collective-permute-start(f32[1,1,16,8192]{3,2,1,0:T(8,128)S(1)} %copy-done.7), channel_id=1, source_target_pairs={{0,13},{1,12},{2,15},{3,14},{4,9},{5,8},{6,11},{7,10},{8,5},{9,4},... | collective-permute-start | bytes 1572872 | tf_op jit(solution)/shard_map/ppermute | solution.py:34
  325.6 76.4 %collective-permute-start.13 = (f32[1,1,16,8192]{3,2,1,0:T(8,128)S(1)}, f32[1,1,16,8192]{3,2,1,0:T(8,128)S(1)}, u32[]{:S(2)}, u32[]{:S(2)}) collective-permute-start(f32[1,1,16,8192]{3,2,1,0:T(8,128)S(1)} %copy-done.6), channel_id=1, source_target_pairs={{0,14},{1,15},{2,12},{3,13},{4,10},{5,11},{6,8},{7,9},{8,6},{9,7},... | collective-permute-start | bytes 1572872 | tf_op jit(solution)/shard_map/ppermute | solution.py:34
  350.1 76.5 %collective-permute-start.14 = (f32[1,1,16,8192]{3,2,1,0:T(8,128)}, f32[1,1,16,8192]{3,2,1,0:T(8,128)S(1)}, u32[]{:S(2)}, u32[]{:S(2)}) collective-permute-start(f32[1,1,16,8192]{3,2,1,0:T(8,128)} %get-tuple-element.294), channel_id=1, source_target_pairs={{0,15},{1,14},{2,13},{3,12},{4,11},{5,10},{6,9},{7,8},{8,7},{9,6},... | collective-permute-start | bytes 1572872 | tf_op jit(solution)/shard_map/ppermute | solution.py:34
  371.9 71.6 %collective-permute-start.15 = (bf16[128,2,1024]{2,1,0:T(2,128)(2,1)}, bf16[128,2,1024]{2,1,0:T(2,128)(2,1)S(1)}, u32[]{:S(2)}, u32[]{:S(2)}) collective-permute-start(bf16[128,2,1024]{2,1,0:T(2,128)(2,1)} %get-tuple-element.328), channel_id=1, source_target_pairs={{12,0},{13,1},{14,2},{15,3},{0,4},{1,5},{2,6},{3,7},{4,8},{5,9},{6... | collective-permute-start | bytes 1572872 | tf_op jit(solution)/shard_map/ppermute | solution.py:42
  373.1 70.4 %collective-permute-start.16 = (bf16[128,2,1024]{2,1,0:T(2,128)(2,1)}, bf16[128,2,1024]{2,1,0:T(2,128)(2,1)S(1)}, u32[]{:S(2)}, u32[]{:S(2)}) collective-permute-start(bf16[128,2,1024]{2,1,0:T(2,128)(2,1)} %get-tuple-element.330), channel_id=1, source_target_pairs={{13,0},{14,1},{15,2},{0,3},{1,4},{2,5},{3,6},{4,7},{5,8},{6,9},{7,... | collective-permute-start | bytes 1572872 | tf_op jit(solution)/shard_map/ppermute | solution.py:42
  374.3 69.3 %collective-permute-start.17 = (bf16[128,2,1024]{2,1,0:T(2,128)(2,1)}, bf16[128,2,1024]{2,1,0:T(2,128)(2,1)S(1)}, u32[]{:S(2)}, u32[]{:S(2)}) collective-permute-start(bf16[128,2,1024]{2,1,0:T(2,128)(2,1)} %get-tuple-element.329), channel_id=1, source_target_pairs={{14,0},{15,1},{0,2},{1,3},{2,4},{3,5},{4,6},{5,7},{6,8},{7,9},{8,1... | collective-permute-start | bytes 1572872 | tf_op jit(solution)/shard_map/ppermute | solution.py:42
  402.0 41.5 %collective-permute-start.18 = (bf16[128,2,1024]{2,1,0:T(2,128)(2,1)}, bf16[128,2,1024]{2,1,0:T(2,128)(2,1)S(1)}, u32[]{:S(2)}, u32[]{:S(2)}) collective-permute-start(bf16[128,2,1024]{2,1,0:T(2,128)(2,1)} %get-tuple-element.331), channel_id=1, source_target_pairs={{15,0},{0,1},{1,2},{2,3},{3,4},{4,5},{5,6},{6,7},{7,8},{8,9},{9,10... | collective-permute-start | bytes 1572872 | tf_op jit(solution)/shard_map/ppermute | solution.py:42
  435.2 8.4 copy-start.3
  452.4 20.9 %copy-start.4 = (bf16[8,128,2,1024]{3,2,1,0:T(2,128)(2,1)}, bf16[8,128,2,1024]{3,2,1,0:T(2,128)(2,1)S(1)}, u32[]{:S(2)}) copy-start(bf16[8,128,2,1024]{3,2,1,0:T(2,128)(2,1)S(1)} %broadcast_select_fusion.4) | copy-start | bytes 12582916
  481.5 173.2 %copy-start.5 = (f32[16,16,64]{2,1,0:T(8,128)S(1)}, f32[16,16,64]{2,1,0:T(8,128)}, u32[]{:S(2)}) copy-start(f32[16,16,64]{2,1,0:T(8,128)} %get-tuple-element.283) | copy-start | bytes 196612
  487.5 5.7 copy-start.1
  519.2 5.7 copy-start.1
  550.8 5.7 copy-start.1
  582.4 5.7 copy-start.1
  608.5 58.3 %copy-start.9 = (f32[16,64]{1,0:T(8,128)S(1)}, f32[16,64]{1,0:T(8,128)}, u32[]{:S(2)}) copy-start(f32[16,64]{1,0:T(8,128)} %get-tuple-element.282) | copy-start | bytes 12292
  609.3 52.3 %all-to-all-start.3 = ((f32[16,1,1024]{2,1,0:T(1,128)}), f32[16,1,1024]{2,1,0:T(1,128)S(1)}, u32[]{:S(2)}, u32[]{:S(2)}) async-start(f32[16,1,1024]{2,1,0:T(1,128)} %reshape.320), calls=%async_computation.4 | async-start | bytes 131072 | tf_op jit(solution)/shard_map/all_to_all | solution.py:129
  661.6 12.1 %all-to-all-start.4 = ((f32[16,1,1024]{2,1,0:T(1,128)}), f32[16,1,1024]{2,1,0:T(1,128)S(1)}, u32[]{:S(2)}, u32[]{:S(2)}) async-start(f32[16,1,1024]{2,1,0:T(1,128)} %reshape.322), calls=%async_computation.5 | async-start | bytes 131072 | tf_op jit(solution)/shard_map/all_to_all | solution.py:136
  673.7 16.2 %all-to-all-start.2 = ((bf16[16,16,512]{2,0,1:T(8,128)(2,1)}), bf16[16,16,512]{2,0,1:T(8,128)(2,1)S(1)}, u32[]{:S(2)}, u32[]{:S(2)}) async-start(bf16[16,16,512]{2,0,1:T(8,128)(2,1)} %copy.53), calls=%async_computation.2 | async-start | bytes 524288 | tf_op jit(solution)/shard_map/all_to_all | solution.py:144
  677.2 307.7 %reduce-scatter.3.cloned.1.call-start = ((), (), s32[]{:S(2)}) async-start(), calls=%async_computation.8 | async-start | bytes 8912896 | tf_op jit(solution)/shard_map/reduce_scatter | solution.py:146
  684.2 14.7 %collective-permute-start.19 = (f32[1,1,16,8192]{3,2,1,0:T(8,128)}, f32[1,1,16,8192]{3,2,1,0:T(8,128)S(1)}, u32[]{:S(2)}, u32[]{:S(2)}) collective-permute-start(f32[1,1,16,8192]{3,2,1,0:T(8,128)} %get-tuple-element.326), channel_id=1, source_target_pairs={{0,1},{1,0},{2,3},{3,2},{4,5},{5,4},{6,7},{7,6},{8,9},{9,8},{10,11... | collective-permute-start | bytes 1572872 | tf_op jit(solution)/shard_map/ppermute | solution.py:34
  684.6 17.9 %collective-permute-start.20 = (f32[1,1,16,8192]{3,2,1,0:T(8,128)}, f32[1,1,16,8192]{3,2,1,0:T(8,128)S(1)}, u32[]{:S(2)}, u32[]{:S(2)}) collective-permute-start(f32[1,1,16,8192]{3,2,1,0:T(8,128)} %get-tuple-element.325), channel_id=1, source_target_pairs={{0,2},{1,3},{2,0},{3,1},{4,6},{5,7},{6,4},{7,5},{8,10},{9,11},{10,... | collective-permute-start | bytes 1572872 | tf_op jit(solution)/shard_map/ppermute | solution.py:34
  686.2 23.3 %collective-permute-start.21 = (f32[1,1,16,8192]{3,2,1,0:T(8,128)}, f32[1,1,16,8192]{3,2,1,0:T(8,128)S(1)}, u32[]{:S(2)}, u32[]{:S(2)}) collective-permute-start(f32[1,1,16,8192]{3,2,1,0:T(8,128)} %get-tuple-element.324), channel_id=1, source_target_pairs={{0,3},{1,2},{2,1},{3,0},{4,7},{5,6},{6,5},{7,4},{8,11},{9,10},{10,... | collective-permute-start | bytes 1572872 | tf_op jit(solution)/shard_map/ppermute | solution.py:34
  686.2 26.9 %collective-permute-start.22 = (f32[1,1,16,8192]{3,2,1,0:T(8,128)}, f32[1,1,16,8192]{3,2,1,0:T(8,128)S(1)}, u32[]{:S(2)}, u32[]{:S(2)}) collective-permute-start(f32[1,1,16,8192]{3,2,1,0:T(8,128)} %get-tuple-element.323), channel_id=1, source_target_pairs={{0,4},{1,5},{2,6},{3,7},{4,0},{5,1},{6,2},{7,3},{8,12},{9,13},{10,... | collective-permute-start | bytes 1572872 | tf_op jit(solution)/shard_map/ppermute | solution.py:34
  688.0 26.3 %collective-permute-start.23 = (f32[1,1,16,8192]{3,2,1,0:T(8,128)}, f32[1,1,16,8192]{3,2,1,0:T(8,128)S(1)}, u32[]{:S(2)}, u32[]{:S(2)}) collective-permute-start(f32[1,1,16,8192]{3,2,1,0:T(8,128)} %get-tuple-element.322), channel_id=1, source_target_pairs={{0,5},{1,4},{2,7},{3,6},{4,1},{5,0},{6,3},{7,2},{8,13},{9,12},{10,... | collective-permute-start | bytes 1572872 | tf_op jit(solution)/shard_map/ppermute | solution.py:34
  698.9 387.8 %reduce-scatter.5.cloned.1.call-start = ((), (), s32[]{:S(2)}) async-start(), calls=%async_computation.9 | async-start | bytes 8912896 | tf_op jit(solution)/shard_map/reduce_scatter | solution.py:146
  699.0 64.0 %collective-permute-start.24 = (f32[1,1,16,8192]{3,2,1,0:T(8,128)}, f32[1,1,16,8192]{3,2,1,0:T(8,128)S(1)}, u32[]{:S(2)}, u32[]{:S(2)}) collective-permute-start(f32[1,1,16,8192]{3,2,1,0:T(8,128)} %get-tuple-element.321), channel_id=1, source_target_pairs={{0,6},{1,7},{2,4},{3,5},{4,2},{5,3},{6,0},{7,1},{8,14},{9,15},{10,... | collective-permute-start | bytes 1572872 | tf_op jit(solution)/shard_map/ppermute | solution.py:34
  702.5 75.8 %collective-permute-start.25 = (f32[1,1,16,8192]{3,2,1,0:T(8,128)}, f32[1,1,16,8192]{3,2,1,0:T(8,128)S(1)}, u32[]{:S(2)}, u32[]{:S(2)}) collective-permute-start(f32[1,1,16,8192]{3,2,1,0:T(8,128)} %get-tuple-element.320), channel_id=1, source_target_pairs={{0,7},{1,6},{2,5},{3,4},{4,3},{5,2},{6,1},{7,0},{8,15},{9,14},{10,... | collective-permute-start | bytes 1572872 | tf_op jit(solution)/shard_map/ppermute | solution.py:34
  709.5 71.0 %collective-permute-start.26 = (f32[1,1,16,8192]{3,2,1,0:T(8,128)}, f32[1,1,16,8192]{3,2,1,0:T(8,128)S(1)}, u32[]{:S(2)}, u32[]{:S(2)}) collective-permute-start(f32[1,1,16,8192]{3,2,1,0:T(8,128)} %get-tuple-element.319), channel_id=1, source_target_pairs={{0,8},{1,9},{2,10},{3,11},{4,12},{5,13},{6,14},{7,15},{8,0},{9,1},... | collective-permute-start | bytes 1572872 | tf_op jit(solution)/shard_map/ppermute | solution.py:34
  713.1 70.8 %collective-permute-start.27 = (f32[1,1,16,8192]{3,2,1,0:T(8,128)}, f32[1,1,16,8192]{3,2,1,0:T(8,128)S(1)}, u32[]{:S(2)}, u32[]{:S(2)}) collective-permute-start(f32[1,1,16,8192]{3,2,1,0:T(8,128)} %get-tuple-element.318), channel_id=1, source_target_pairs={{0,9},{1,8},{2,11},{3,10},{4,13},{5,12},{6,15},{7,14},{8,1},{9,0},... | collective-permute-start | bytes 1572872 | tf_op jit(solution)/shard_map/ppermute | solution.py:34
  714.3 144.1 %collective-permute-start.28 = (f32[1,1,16,8192]{3,2,1,0:T(8,128)}, f32[1,1,16,8192]{3,2,1,0:T(8,128)S(1)}, u32[]{:S(2)}, u32[]{:S(2)}) collective-permute-start(f32[1,1,16,8192]{3,2,1,0:T(8,128)} %get-tuple-element.317), channel_id=1, source_target_pairs={{0,10},{1,11},{2,8},{3,9},{4,14},{5,15},{6,12},{7,13},{8,2},{9,3},... | collective-permute-start | bytes 1572872 | tf_op jit(solution)/shard_map/ppermute | solution.py:34
  762.9 120.7 %collective-permute-start.29 = (f32[1,1,16,8192]{3,2,1,0:T(8,128)}, f32[1,1,16,8192]{3,2,1,0:T(8,128)S(1)}, u32[]{:S(2)}, u32[]{:S(2)}) collective-permute-start(f32[1,1,16,8192]{3,2,1,0:T(8,128)} %get-tuple-element.316), channel_id=1, source_target_pairs={{0,11},{1,10},{2,9},{3,8},{4,15},{5,14},{6,13},{7,12},{8,3},{9,2},... | collective-permute-start | bytes 1572872 | tf_op jit(solution)/shard_map/ppermute | solution.py:34
  778.3 106.2 %collective-permute-start.30 = (f32[1,1,16,8192]{3,2,1,0:T(8,128)}, f32[1,1,16,8192]{3,2,1,0:T(8,128)S(1)}, u32[]{:S(2)}, u32[]{:S(2)}) collective-permute-start(f32[1,1,16,8192]{3,2,1,0:T(8,128)} %get-tuple-element.315), channel_id=1, source_target_pairs={{0,12},{1,13},{2,14},{3,15},{4,8},{5,9},{6,10},{7,11},{8,4},{9,5},... | collective-permute-start | bytes 1572872 | tf_op jit(solution)/shard_map/ppermute | solution.py:34
  780.6 104.7 %collective-permute-start.31 = (f32[1,1,16,8192]{3,2,1,0:T(8,128)}, f32[1,1,16,8192]{3,2,1,0:T(8,128)S(1)}, u32[]{:S(2)}, u32[]{:S(2)}) collective-permute-start(f32[1,1,16,8192]{3,2,1,0:T(8,128)} %get-tuple-element.314), channel_id=1, source_target_pairs={{0,13},{1,12},{2,15},{3,14},{4,9},{5,8},{6,11},{7,10},{8,5},{9,4},... | collective-permute-start | bytes 1572872 | tf_op jit(solution)/shard_map/ppermute | solution.py:34
  783.9 102.2 %collective-permute-start.32 = (f32[1,1,16,8192]{3,2,1,0:T(8,128)}, f32[1,1,16,8192]{3,2,1,0:T(8,128)S(1)}, u32[]{:S(2)}, u32[]{:S(2)}) collective-permute-start(f32[1,1,16,8192]{3,2,1,0:T(8,128)} %get-tuple-element.313), channel_id=1, source_target_pairs={{0,14},{1,15},{2,12},{3,13},{4,10},{5,11},{6,8},{7,9},{8,6},{9,7},... | collective-permute-start | bytes 1572872 | tf_op jit(solution)/shard_map/ppermute | solution.py:34
  858.4 28.6 %collective-permute-start.33 = (f32[1,1,16,8192]{3,2,1,0:T(8,128)}, f32[1,1,16,8192]{3,2,1,0:T(8,128)S(1)}, u32[]{:S(2)}, u32[]{:S(2)}) collective-permute-start(f32[1,1,16,8192]{3,2,1,0:T(8,128)} %get-tuple-element.312), channel_id=1, source_target_pairs={{0,15},{1,14},{2,13},{3,12},{4,11},{5,10},{6,9},{7,8},{8,7},{9,6},... | collective-permute-start | bytes 1572872 | tf_op jit(solution)/shard_map/ppermute | solution.py:34
Sparse Core Ops, SparseCore 0:
  699.0 232.0 reduce-scatter.2
  985.1 101.6 reduce-scatter.4
